TPU v7x, 128 devices: a whole 4x4x4 slice. The times are simulated.
128 devices in a mesh: tm: 8 (over x, core), dom: 16 (over z, y).
Axes of the slice: x: 4, y: 4, z: 4, core: 2. Of those that a mesh axis runs over, the one named last changes fastest.
Arguments:
- features: bfloat16 [16, 8192, 128], P('tm', 'dom'), may hold values from -6 to 6
- tile_values: bfloat16 [16, 64, 16, 4, 128, 128], P('tm', 'dom'), may hold values from -0.09375 to 0.09375
- tile_cols: int32 [16, 64, 16, 4], P('tm', 'dom'), may hold values from 0 to 3
- tile_count: int32 [16, 64, 16], P('tm', 'dom'), may hold values from 0 to 4, as said below
- hidden_start: float32 [8192, 512], P('dom'), may hold values from -4 to 4
- w_graph: bfloat16 [128, 512], replicated, may hold values from -0.5 to 0.5
- w_input: bfloat16 [512, 1536], replicated, may hold values from -0.25 to 0.25
- w_hidden: bfloat16 [512, 1536], replicated, may hold values from -0.25 to 0.25
- update_bias: float32 [512], replicated, may hold values from -1 to 4
Outputs:
- hidden_seq: bfloat16 [16, 8192, 512], P('tm', 'dom')
Inputs may be any that keep to these rules, and one draw needn't show every extreme that they name: `tile_count`: number of live slots; for each row block the entry of its own partition is 4.
All inputs are finite; a program needn't handle non-finite values.
Results may differ from a plain program's by a relative error of at most 0.0052.
Values may be sent and summed in bfloat16 or wider, within the bound.
A program may use at most 128 MiB of HBM per device.

v0:
```python
import functools

import jax
import jax.numpy as jnp
from jax import lax
from jax.experimental import pallas as pl
from jax.experimental.pallas import tpu as pltpu
from jax.sharding import PartitionSpec as P

MESH = pl.DeviceIdType.MESH
SIDE = 4
BF = jnp.bfloat16
F32 = jnp.float32


ORDER = (
    "P0", "Q0", "P1", "E10", "E1b0", "E30", "E20", "E40", "U40", "U20", "E50", "E11",
    "U000", "E60", "E1b1", "U50", "F30", "Q1", "F00", "U60", "U70", "F10", "U80", "E31",
    "F20", "U90", "X0", "E41", "U001", "U41", "E51", "U51", "G10", "G20", "E21", "U21",
    "E61", "G30", "F31", "U71", "J0", "F11", "U81", "F01", "U61", "F21", "U91", "X1",
)
UNITS = {
    "U00": ((0, 0),),
    "U2": ((0, 3), (0, 1), (3, 0), (1, 0)),
    "U4": ((3, 3),),
    "U5": ((1, 3), (3, 1), (1, 1)),
    "U6": ((0, 2), (2, 0)),
    "U7": ((2, 3), (3, 2)),
    "U8": ((2, 1), (1, 2)),
    "U9": ((2, 2),),
}


def kernel(tms, feat, tiles, cols_in, cnt_in, h0, wg, wi, wh, bias, out, *scratch):
    nslot = SIDE * SIDE
    xs = [scratch[s * nslot : (s + 1) * nslot] for s in range(2)]
    (
        tbuf, acc, ax, mine, halves, gx, gx_own, state, state_own, stage, moved, stage_own,
        wgv, wiv, whv, biasv, biasg, graph, cols, cnt,
        ring_send, ring_recv, tile_sem, load_sem, ax_send, ax_recv, half_send, half_recv,
        move_send, move_recv, out_send, out_recv, out_local,
    ) = scratch[2 * nslot :]
    nb = feat.shape[1]
    half = nb // 2
    blk = feat.shape[2]
    kp = tiles.shape[3]
    hid = wg.shape[1]
    share = state.shape[0]
    hs = tms // 2
    wide = hs * share

    me = lax.axis_index("tm")
    dom = lax.axis_index("dom")
    core = me % 2
    chip = me // 2
    partner = me + 1 - 2 * core
    z = dom // SIDE
    y = dom % SIDE

    def at(dz, dy):
        return ((z + dz) % SIDE) * SIDE + (y + dy) % SIDE

    barrier = pltpu.get_barrier_semaphore()
    for dz, dy in ((0, 1), (0, SIDE - 1), (1, 0), (SIDE - 1, 0)):
        pl.semaphore_signal(barrier, inc=1, device_id=(me, at(dz, dy)), device_id_type=MESH)
    for o in range(1, tms):
        pl.semaphore_signal(barrier, inc=1, device_id=((me + o) % tms, dom), device_id_type=MESH)

    own = [pltpu.make_async_copy(feat.at[s], xs[s][0].at[pl.ds(0, nb)], load_sem.at[s]) for s in range(2)]
    loads = [
        pltpu.make_async_copy(wg, wgv, load_sem.at[2]),
        pltpu.make_async_copy(wi, wiv, load_sem.at[3]),
        pltpu.make_async_copy(wh, whv, load_sem.at[4]),
        pltpu.make_async_copy(bias, biasv, load_sem.at[5]),
        pltpu.make_async_copy(h0.at[pl.ds(me * share, share)], state, load_sem.at[6]),
    ]
    own.append(pltpu.make_async_copy(cols_in, cols, load_sem.at[7]))
    own.append(pltpu.make_async_copy(cnt_in, cnt, load_sem.at[8]))
    for c in own:
        c.start()

    def tile_copy(slot):
        return pltpu.make_async_copy(
            tiles.at[:, :, at(slot // SIDE, slot % SIDE)], tbuf.at[slot], tile_sem.at[slot]
        )

    pl.semaphore_wait(barrier, 3 + tms)

    def slot_of(h, df, dg):
        return dg * SIDE + df if h == 0 else df * SIDE + dg

    def to(h, first, way):
        step = 1 if way == 0 else SIDE - 1
        along_y = first == (h == 0)
        return at(0, step) if along_y else at(step, 0)

    def ring(s, h, ident, src, dst_slot, lo, n, target):
        i = (s * 2 + h) * 20 + ident
        return pltpu.make_async_remote_copy(
            src_ref=src,
            dst_ref=xs[s][dst_slot].at[pl.ds(lo, n)],
            send_sem=ring_send.at[i],
            recv_sem=ring_recv.at[i],
            device_id=(me, target),
            device_id_type=MESH,
        )

    def held(s, slot, lo, n):
        return xs[s][slot].at[pl.ds(lo, n)]

    copies = []
    far = (SIDE - 1, 1)
    p1, p1f, p2, p2f = {}, {}, {}, {}
    for s in range(2):
        for h in range(2):
            lo = h * half
            mid = (lo, lo + half // 2)
            for way in range(2):
                first, second = to(h, True, way), to(h, False, way)
                src = feat.at[s, pl.ds(lo, half)]
                p1[s, h, way] = ring(s, h, way, src, slot_of(h, far[way], 0), lo, half, first)
                p1f[s, h, way] = ring(
                    s, h, 2 + way, held(s, slot_of(h, far[way], 0), mid[way], half // 2),
                    slot_of(h, 2, 0), mid[way], half // 2, first,
                )
                for df in range(SIDE):
                    src = feat.at[s, pl.ds(lo, half)] if df == 0 else held(s, slot_of(h, df, 0), lo, half)
                    p2[s, h, df, way] = ring(
                        s, h, 4 + 2 * df + way, src, slot_of(h, df, far[way]), lo, half, second
                    )
                    p2f[s, h, df, way] = ring(
                        s, h, 12 + 2 * df + way, held(s, slot_of(h, df, far[way]), mid[way], half // 2),
                        slot_of(h, df, 2), mid[way], half // 2, second,
                    )
    both = [(h, w) for w in range(2) for h in range(2)]

    def start(table, s, *df):
        for h, w in both:
            c = table[(s, h) + df + (w,)]
            c.start()
            copies.append(c)

    def arrived(table, s, *df):
        for h, w in both:
            table[(s, h) + df + (w,)].wait_recv()

    early = {"P": lambda s: start(p1, s), "Q": lambda s: start(p2, s, 0)}

    def unit(s, *pairs):
        slots = [dz * SIDE + dy for dz, dy in pairs]
        parts = [at(dz, dy) for dz, dy in pairs]
        if s == 0:
            for slot in slots:
                tile_copy(slot).wait()

        def block(r):
            left, right = [], []
            for slot, part in zip(slots, parts):
                n = cnt[s, r, part]
                for k in range(kp):
                    left.append(tbuf[slot, s, r, k])
                    right.append(xs[s][slot][jnp.where(k < n, cols[s, r, k, part], nb)])
            acc[s, r] += jnp.dot(
                jnp.concatenate(left, axis=1), jnp.concatenate(right, axis=0), preferred_element_type=F32
            )

        def body(i, carry):
            block(2 * i)
            block(2 * i + 1)
            return carry

        lax.fori_loop(0, nb // 2, body, 0)

    peers = [(d, k) for d in (2, 1, hs - 1, 0) for k in range(2) if d + k > 0]

    def peer(d, k):
        return 2 * ((chip + d) % hs) + (core + k) % 2

    def exchange_copies(s):
        return [
            pltpu.make_async_remote_copy(
                src_ref=ax.at[s, peer(d, k)],
                dst_ref=mine.at[s, me],
                send_sem=ax_send.at[s, 2 * d + k],
                recv_sem=ax_recv.at[s, 2 * d + k],
                device_id=(peer(d, k), dom),
                device_id_type=MESH,
            )
            for d, k in peers
        ]

    def half_copy(s):
        return pltpu.make_async_remote_copy(
            src_ref=ax.at[s, pl.ds((1 - core) * hs, hs)],
            dst_ref=halves.at[s, core],
            send_sem=half_send.at[s],
            recv_sem=half_recv.at[s],
            device_id=(partner, dom),
            device_id_type=MESH,
        )

    def exchange(s):
        for r in range(nb):
            v = acc[s, r].astype(BF)
            for q in range(blk // share):
                ax[s, r * (blk // share) + q] = v[q * share : (q + 1) * share]
        half_copy(s).start()
        copies.append(half_copy(s))

        @pl.when(me < tms - 1 - s)
        def _():
            for c in exchange_copies(s):
                c.start()

        mine[s, me] = ax[s, me]
        halves[s, core] = ax[s, pl.ds(core * hs, hs)]

    width = min(256, hid)
    pairs_of = 3 * hid // (2 * width)

    def graph_of(rows):
        rows = rows.reshape(-1, feat.shape[3])
        value = jnp.dot(rows, wgv[...], preferred_element_type=F32)
        graph[: rows.shape[0]] = jnp.maximum(value, 0.0).astype(BF)

    def gates(put, n, lo=0, hi=pairs_of, unroll=False):
        def one(j):
            columns = pl.ds(j * width if unroll else pl.multiple_of(j * width, width), width)
            value = jnp.dot(graph[:n], wiv[:, columns], preferred_element_type=F32)
            put(columns, value + biasg[:, columns])

        def body(j, carry):
            one(2 * j)
            one(2 * j + 1)
            return carry

        if unroll:
            for j in range(lo, hi):
                body(j, 0)
        else:
            lax.fori_loop(lo, hi, body, 0)

    def chain_gates(s, lo=0, hi=pairs_of):
        if lo == 0:
            for (d, k), c in zip(peers, exchange_copies(s)):
                @pl.when(peer(hs - d, k) < tms - 1 - s)
                def _(c=c):
                    c.wait_recv()
            graph_of(mine[s, : tms - 1 - s])

        def put(columns, value):
            gx[s, : (tms - 1 - s) * share, columns] = value

        gates(put, (tms - 1 - s) * share, lo, hi, unroll=s == 1)

    def own_gates(first, n):
        def put(columns, value):
            gx_own[first : first + n, columns] = value

        gates(put, n)

    def scale_weights():
        rows = hid // 16

        def body(i, carry):
            r = pl.ds(pl.multiple_of(i * rows, rows), rows)
            whv[r] = whv[r] * 0.5
            wiv[r, : 2 * hid] = wiv[r, : 2 * hid] * 0.5
            return carry

        lax.fori_loop(0, 16, body, 0)
        biasg[...] = jnp.zeros_like(biasg)
        biasg[:, hid : 2 * hid] = biasv[...] * 0.5

    def cell(now, st, gates_at, put, done=None):
        n = now.shape[0]
        for j in range(hid // width):
            c = slice(j * width, (j + 1) * width)

            def gate(g):
                col = slice(g * hid + j * width, g * hid + (j + 1) * width)
                return col, jnp.dot(now, whv[:, col], preferred_element_type=F32)

            col_r, gh_r = gate(0)
            col_c, gh_c = gate(2)
            col_u, gh_u = gate(1)
            for q in range(n // share):
                rows = slice(q * share, (q + 1) * share)
                reset = jnp.tanh(gates_at(rows, col_r) + gh_r[rows])
                part = gh_c[rows]
                cand = jnp.tanh(gates_at(rows, col_c) + (part + reset * part))
                update = jnp.tanh(gates_at(rows, col_u) + gh_u[rows])
                diff = 0.5 * (st[rows, c] - cand)
                new = (cand + diff) + update * diff
                st[rows, c] = new
                put(rows, c, new.astype(BF))
        if done is not None:
            done()


    def move_copy(q):
        return pltpu.make_async_remote_copy(
            src_ref=stage.at[q],
            dst_ref=moved.at[pl.ds((me % hs) * share, share)],
            send_sem=move_send.at[q],
            recv_sem=move_recv.at[me % hs],
            device_id=(2 * q + me // hs, dom),
            device_id_type=MESH,
        )

    def chain(par, sec, q=None):
        base = pl.multiple_of(sec * share, share)

        def gates_at(rows, col):
            return gx[par, pl.ds(base, share), col]

        def put(rows, c, value):
            if q is not None:
                stage[q, rows, c] = value

        def done():
            target = 2 * q + me // hs

            @pl.when(target == me)
            def _():
                moved[pl.ds(pl.multiple_of((me % hs) * share, share), share)] = stage[q]

            @pl.when(target != me)
            def _():
                move_copy(q).start()

        cell(state[...].astype(BF), state, gates_at, put, None if q is None else done)

    def four(i, carry):
        chain(1, 2 * i)
        chain(0, 2 * i + 1)
        chain(1, 2 * i + 1)
        chain(0, 2 * i + 2, i + 1)
        return carry

    for word in ORDER[:3]:
        early[word[0]](int(word[1]))
    for slot in range(nslot):
        tile_copy(slot).start()
    for c in loads:
        c.start()
    for s in range(2):
        for slot in range(nslot):
            xs[s][slot][nb] = jnp.zeros((blk, feat.shape[3]), BF)
    acc[...] = jnp.zeros_like(acc)
    for c in own:
        c.wait()

    def step(kind, s):
        if kind == "P":
            start(p1, s)
        elif kind == "Q":
            start(p2, s, 0)
        elif kind == "E1":
            arrived(p1, s)
            start(p1f, s)
        elif kind == "E1b":
            start(p2, s, 3)
            start(p2, s, 1)
        elif kind == "E3":
            arrived(p1f, s)
            start(p2, s, 2)
        elif kind[0] == "E":
            d = {"E2": 0, "E4": 3, "E5": 1, "E6": 2}[kind]
            arrived(p2, s, d)
            start(p2f, s, d)
        elif kind[0] == "F":
            arrived(p2f, s, int(kind[1]))
        elif kind == "X":
            exchange(s)
            if s == 0:
                for c in loads:
                    c.wait()
                scale_weights()
        elif kind[0] == "G":
            chain_gates(0, int(kind[1]) - 1, int(kind[1]))
        elif kind == "J":
            half_copy(0).wait_recv()
            graph_of(halves[0, 1])
            own_gates(2 * wide, wide)
        else:
            unit(s, *UNITS[kind])

    for word in ORDER[3:]:
        step(word[:-1], int(word[-1]))
    chain(0, 0, 0)
    chain_gates(1)
    lax.fori_loop(0, hs - 1, four, 0)

    half_copy(1).wait_recv()
    graph_of(halves[1])
    own_gates(0, 2 * wide)
    for k in range(hs):
        @pl.when(core * hs + k != me)
        def _(k=k):
            pltpu.make_async_remote_copy(
                src_ref=stage.at[0],
                dst_ref=moved.at[pl.ds(k * share, share)],
                send_sem=move_send.at[0],
                recv_sem=move_recv.at[k],
                device_id=(partner, dom),
                device_id_type=MESH,
            ).wait_recv()

    def sent_copy(j, src):
        return pltpu.make_async_remote_copy(
            src_ref=src,
            dst_ref=out.at[j % 2, pl.ds(core * wide, wide)],
            send_sem=out_send.at[j],
            recv_sem=out_recv.at[j],
            device_id=(partner, dom),
            device_id_type=MESH,
        )

    def kept_copy(j, src):
        return pltpu.make_async_copy(src, out.at[j % 2, pl.ds(core * wide, wide)], out_local.at[j])

    def deliver(j, src):
        @pl.when(core == j // 2)
        def _():
            kept_copy(j, src).start()

        @pl.when(core != j // 2)
        def _():
            sent_copy(j, src).start()

    deliver(0, moved)
    state_own[...] = moved[...].astype(F32)

    def own_step(j, carry):
        base = pl.multiple_of((2 * (j - 1) % 3) * wide, wide)

        def gates_at(rows, col):
            return gx_own[pl.ds(base + rows.start, share), col]

        def put(rows, c, value):
            stage_own[j - 1, rows, c] = value

        def done():
            deliver(j, stage_own.at[j - 1])

        cell(state_own[...].astype(BF), state_own, gates_at, put, done)
        return carry

    lax.fori_loop(1, 4, own_step, 0)

    for c in copies:
        c.wait_send()
    for s in range(2):
        @pl.when(me < tms - 1 - s)
        def _(s=s):
            for c in exchange_copies(s):
                c.wait_send()
    for q in range(hs):
        @pl.when(2 * q + me // hs != me)
        def _(q=q):
            move_copy(q).wait_send()
    for j in range(4):
        src = moved if j == 0 else stage_own.at[j - 1]

        @pl.when(core == j // 2)
        def _(j=j, src=src):
            kept_copy(j, src).wait()
            sent_copy(j, src).wait_recv()

        @pl.when(core != j // 2)
        def _(j=j, src=src):
            sent_copy(j, src).wait_send()


def per_device(tms, features, tile_values, tile_cols, tile_count, hidden_start, w_graph, w_input, w_hidden, update_bias):
    snaps, nodes, feats = features.shape
    nb, kp, blk = tile_values.shape[1], tile_values.shape[3], tile_values.shape[4]
    hid = w_graph.shape[1]
    share = nodes // tms
    nslot = SIDE * SIDE
    hbm = pl.BlockSpec(memory_space=pltpu.HBM)
    dma = pltpu.SemaphoreType.DMA
    scratch = [pltpu.VMEM((nb + 1, blk, feats), BF) for _ in range(2 * nslot)] + [
        pltpu.VMEM((nslot, 2, nb, kp, blk, blk), BF),
        pltpu.VMEM((2, nb, blk, feats), F32),
        pltpu.VMEM((2, tms, share, feats), BF),
        pltpu.VMEM((2, tms, share, feats), BF),
        pltpu.VMEM((2, 2, tms // 2, share, feats), BF),
        pltpu.VMEM((2, tms * share, 3 * hid), F32),
        pltpu.VMEM((3 * nodes // 2, 3 * hid), F32),
        pltpu.VMEM((share, hid), F32),
        pltpu.VMEM((nodes // 2, hid), F32),
        pltpu.VMEM((tms // 2, share, hid), BF),
        pltpu.VMEM((nodes // 2, hid), BF),
        pltpu.VMEM((3, nodes // 2, hid), BF),
        pltpu.VMEM(w_graph.shape, BF),
        pltpu.VMEM(w_input.shape, BF),
        pltpu.VMEM(w_hidden.shape, BF),
        pltpu.VMEM((1, hid), F32),
        pltpu.VMEM((1, 3 * hid), F32),
        pltpu.VMEM((tms * share, hid), BF),
        pltpu.SMEM((2, nb, kp, nslot), jnp.int32),
        pltpu.SMEM((2, nb, nslot), jnp.int32),
        dma((80,)),
        dma((80,)),
        dma((nslot,)),
        dma((9,)),
        dma((2, tms)),
        dma((2, tms)),
        dma((2,)),
        dma((2,)),
        dma((tms // 2,)),
        dma((tms // 2,)),
        dma((4,)),
        dma((4,)),
        dma((4,)),
    ]
    call = pl.pallas_call(
        functools.partial(kernel, tms),
        out_shape=jax.ShapeDtypeStruct((snaps, nodes, hid), BF),
        in_specs=[hbm] * 9,
        out_specs=pl.BlockSpec(memory_space=pl.ANY),
        scratch_shapes=scratch,
        compiler_params=pltpu.CompilerParams(
            collective_id=0, has_side_effects=True, vmem_limit_bytes=44 << 20
        ),
    )
    operands = (
        features.reshape(snaps, nb, blk, feats),
        tile_values,
        tile_cols.transpose(0, 1, 3, 2),
        tile_count,
        hidden_start,
        w_graph,
        w_input,
        w_hidden,
        update_bias.reshape(1, hid),
    )
    return call(*(pltpu.with_memory_space_constraint(v, pltpu.HBM) for v in operands))


def solution(mesh):
    placed = (
        P("tm", "dom", None),
        P("tm", "dom", None, None, None, None),
        P("tm", "dom", None, None),
        P("tm", "dom", None),
        P("dom", None),
        P(),
        P(),
        P(),
        P(),
    )
    return jax.shard_map(
        functools.partial(per_device, mesh.shape["tm"]),
        mesh=mesh,
        in_specs=placed,
        out_specs=P("tm", "dom", None),
        check_vma=False,
    )
```

profile of v0, /device:TPU:7, one launch (start us, length us, event | category | flops | bytes accessed | tf_op | source)
XLA Modules:
  0.0 53.1 jit_solution(2606098479647006787)
XLA Ops:
  0.0 52.1 %shard_map.91 = bf16[2,512,512]{2,1,0:T(8,128)(2,1)S(1)} custom-call(bf16[2,4,128,128]{3,2,1,0:T(8,128)(2,1)} %bitcast.3, bf16[2,4,16,4,128,128]{5,4,3,2,1,0:T(8,128)(2,1)} %tiles.1, s32[2,4,4,16]{3,2,1,0:T(4,128)} %bitcast.4, s32[2,4,16]{2,1,0:T(4,128)} %cnt_in.1, f32[512,512]{1,0:T(8,128)} %h0.1, bf16[128,512]{1,0:T(8,128)(2,1)} %wg.1, ...), custom_call_target="tpu_custom_call" | custom-call | tf_op jit(solution)/shard_map/pallas_call | solution.py:540
  52.1 1.0 %copy.11 = bf16[2,512,512]{2,1,0:T(8,128)(2,1)} copy(bf16[2,512,512]{2,1,0:T(8,128)(2,1)S(1)} %shard_map.91) | data formatting | bytes 2097152
where the time goes:
time: 53.2 us; the launch traced here: 53.1 us
  Pallas kernels  52.1 us (98%)
  local copies, waits for them, and re-layouts  0.97 us (2%)
    pallas_call x1, Pallas kernels, per_device(): call(*(pltpu.with_memory_space_constraint(v, pltpu.HBM) for v in operands))  52.1 us

commit v1 on v0

--- a/solution.py
+++ b/solution.py
@@ -14,10 +14,7 @@
 
 
 ORDER = (
-    "P0", "Q0", "P1", "E10", "E1b0", "E30", "E20", "E40", "U40", "U20", "E50", "E11",
-    "U000", "E60", "E1b1", "U50", "F30", "Q1", "F00", "U60", "U70", "F10", "U80", "E31",
-    "F20", "U90", "X0", "E41", "U001", "U41", "E51", "U51", "G10", "G20", "E21", "U21",
-    "E61", "G30", "F31", "U71", "J0", "F11", "U81", "F01", "U61", "F21", "U91", "X1",
+    "P0", "Q0", "P1", "E10", "U000", "E1b0", "E20", "E30", "U20", "E11", "E40", "U001", "E50", "U50", "Q1", "E60", "E1b1", "F30", "F00", "F10", "U40", "U80", "E21", "U60", "E31", "U70", "F20", "U90", "X0", "U21", "E41", "U41", "E51", "U51", "F01", "U61", "G10", "E61", "G20", "G30", "F31", "U71", "F11", "J0", "U81", "F21", "U91", "X1",
 )
 UNITS = {
     "U00": ((0, 0),),
@@ -144,6 +141,13 @@
         for h, w in both:
             table[(s, h) + df + (w,)].wait_recv()
 
+    def relay(table, onward, s, *df):
+        for h, w in both:
+            table[(s, h) + df + (w,)].wait_recv()
+            c = onward[(s, h) + df + (w,)]
+            c.start()
+            copies.append(c)
+
     early = {"P": lambda s: start(p1, s), "Q": lambda s: start(p2, s, 0)}
 
     def unit(s, *pairs):
@@ -357,8 +361,7 @@
         elif kind == "Q":
             start(p2, s, 0)
         elif kind == "E1":
-            arrived(p1, s)
-            start(p1f, s)
+            relay(p1, p1f, s)
         elif kind == "E1b":
             start(p2, s, 3)
             start(p2, s, 1)
@@ -367,8 +370,7 @@
             start(p2, s, 2)
         elif kind[0] == "E":
             d = {"E2": 0, "E4": 3, "E5": 1, "E6": 2}[kind]
-            arrived(p2, s, d)
-            start(p2f, s, d)
+            relay(p2, p2f, s, d)
         elif kind[0] == "F":
             arrived(p2f, s, int(kind[1]))
         elif kind == "X":

time: 53.2 us -> 53.2 us (level)
  no operation moved by 1% of the time
where the time goes in v1:
time: 53.2 us; the launch traced here: 53.1 us
  Pallas kernels  52.1 us (98%)
  local copies, waits for them, and re-layouts  0.97 us (2%)
    pallas_call x1, Pallas kernels, per_device(): call(*(pltpu.with_memory_space_constraint(v, pltpu.HBM) for v in operands))  52.1 us

profile of v1, /device:TPU:7, one launch (start us, length us, event | category | flops | bytes accessed | tf_op | source)
XLA Modules:
  0.0 53.1 jit_solution(4168698082697538294)
XLA Ops:
  0.0 52.1 %shard_map.91 = bf16[2,512,512]{2,1,0:T(8,128)(2,1)S(1)} custom-call(bf16[2,4,128,128]{3,2,1,0:T(8,128)(2,1)} %bitcast.3, bf16[2,4,16,4,128,128]{5,4,3,2,1,0:T(8,128)(2,1)} %tiles.1, s32[2,4,4,16]{3,2,1,0:T(4,128)} %bitcast.4, s32[2,4,16]{2,1,0:T(4,128)} %cnt_in.1, f32[512,512]{1,0:T(8,128)} %h0.1, bf16[128,512]{1,0:T(8,128)(2,1)} %wg.1, ...), custom_call_target="tpu_custom_call" | custom-call | tf_op jit(solution)/shard_map/pallas_call | solution.py:542
  52.1 1.0 %copy.11 = bf16[2,512,512]{2,1,0:T(8,128)(2,1)} copy(bf16[2,512,512]{2,1,0:T(8,128)(2,1)S(1)} %shard_map.91) | data formatting | bytes 2097152
